TPU v7x, 32 devices: a whole 2x2x4 slice. The times are simulated.
32 devices in a mesh: cells: 8 (over z, x), seq: 4 (over y, core).
Axes of the slice: x: 2, y: 2, z: 4, core: 2. Of those that a mesh axis runs over, the one named last changes fastest.
Arguments:
- cell_tokens: bfloat16 [8, 1280, 1120], P('cells', 'seq'), may hold values from -6 to 6
- drop_counts: int32 [8], P('cells'), may hold values from 0 to 4, as said below
- lengths: int32 [8], P('cells'), may hold values from 640 to 1280, as said below
- ln_gain: bfloat16 [2, 1120], replicated, may hold values from 0.25 to 1.75
- ln_shift: bfloat16 [2, 1120], replicated, may hold values from -1.1953125 to 1.1953125
- w_qkv: bfloat16 [3, 1120, 1120], P(None, None, 'seq'), may hold values from -0.1875 to 0.1875
- qv_bias: bfloat16 [2, 1120], P(None, 'seq'), may hold values from -0.29882812 to 0.29882812
- w_out: bfloat16 [1120, 1120], P('seq'), may hold values from -1.5 to 1.5
- out_bias: bfloat16 [2, 1120], replicated, may hold values from -1.1953125 to 1.1953125
- w_up: bfloat16 [4480, 1120], P('cells', 'seq'), may hold values from -0.1875 to 0.1875
- up_bias: bfloat16 [4480], replicated, may hold values from -1.1953125 to 1.1953125
- w_down: bfloat16 [4480, 1120], P('cells', 'seq'), may hold values from -0.09375 to 0.09375
- out_grad: bfloat16 [8, 1280, 1120], P('cells', 'seq'), may hold values from -6 to 6
Outputs:
- block_out: bfloat16 [8, 1280, 1120], P('cells', 'seq')
- in_grad: float32 [8, 1280, 1120], P('cells', 'seq')
- d_ln_gain: float32 [2, 1120], replicated
- d_ln_shift: float32 [2, 1120], replicated
- d_qkv: float32 [3, 1120, 1120], P(None, None, 'seq')
- d_qv_bias: float32 [2, 1120], P(None, 'seq')
- d_out: float32 [1120, 1120], P('seq')
- d_out_bias: float32 [2, 1120], replicated
- d_up: float32 [4480, 1120], P('cells', 'seq')
- d_up_bias: float32 [4480], replicated
- d_down: float32 [4480, 1120], P('cells', 'seq')
Inputs may be any that keep to these rules, and one draw needn't show every extreme that they name: `drop_counts`: one sentence in every draw masks its first 4 positions as keys and one masks none. `lengths`: in every draw one sentence is 1280 long and one is 640 long.
All inputs are finite; a program needn't handle non-finite values.
Results may differ from a plain program's by a relative error of at most 0.012.
The roundings to bfloat16 on the way count: a program that leaves them out, or rounds other values in their place, can miss the bound.
Values may be sent and summed in bfloat16 or wider, within the bound.
A program may use at most 256 MiB of HBM per device.

v0:
```python
import math
import jax
import jax.numpy as jnp
from jax import lax
from jax.sharding import PartitionSpec as P

HEADS = 20
HD = 56
QBLOCK = 640
epsilon = 1e-05
masked_score = -1e30


def layer_norm(rows, gain, shift):
    centre = jnp.mean(rows, axis=-1, keepdims=True)
    offsets = rows - centre
    spread = jnp.mean(offsets * offsets, axis=-1, keepdims=True)
    return offsets * lax.rsqrt(spread + epsilon) * gain + shift


def gelu_tanh(values):
    return jax.nn.gelu(values, approximate=True)


def visible(drop_counts, lengths, start_row, row_count, key_count):
    query_place = start_row + jnp.arange(row_count, dtype=jnp.int32)[:, None]
    key_place = jnp.arange(key_count, dtype=jnp.int32)[None, :]
    dropped = drop_counts[:, None, None, None]
    limits = lengths[:, None, None, None]
    return (
        (key_place <= query_place)
        & (key_place < limits)
        & ((key_place >= dropped) | (key_place == query_place))
    )


def attend(packed, drop_counts, lengths, scale):
    queries = packed[:, :, :, 0]
    keys_all = packed[:, :, :, 1]
    values = packed[:, :, :, 2]
    outputs = []
    log_sums = []
    for start_row in range(0, queries.shape[1], QBLOCK):
        end_row = start_row + QBLOCK
        scores = (
            jnp.einsum(
                "cqhe,ckhe->chqk",
                queries[:, start_row:end_row],
                keys_all[:, :end_row],
                preferred_element_type=jnp.float32,
            )
            * scale
        )
        allowed = visible(drop_counts, lengths, start_row, QBLOCK, end_row)
        scores = jnp.where(allowed, scores, masked_score)
        largest = jnp.max(scores, axis=-1, keepdims=True)
        weights = jnp.where(allowed, jnp.exp(scores - largest), 0.0)
        totals = jnp.sum(weights, axis=-1, keepdims=True)
        probs = (weights / totals).astype(jnp.bfloat16)
        piece_out = jnp.einsum(
            "chqk,ckhe->cqhe", probs, values[:, :end_row], preferred_element_type=jnp.float32
        )
        outputs.append(piece_out.astype(jnp.bfloat16))
        log_sums.append(jnp.transpose((largest + jnp.log(totals))[..., 0], (0, 2, 1)))
    return (jnp.concatenate(outputs, axis=1), jnp.concatenate(log_sums, axis=1))


def attend_back(packed, grad_out, log_sums, drop_counts, lengths, scale):
    queries = packed[:, :, :, 0]
    keys_all = packed[:, :, :, 1]
    values = packed[:, :, :, 2]
    grad_query = []
    grad_key = jnp.zeros(keys_all.shape, jnp.float32)
    grad_value = jnp.zeros(values.shape, jnp.float32)
    for start_row in range(0, queries.shape[1], QBLOCK):
        end_row = start_row + QBLOCK
        scores = (
            jnp.einsum(
                "cqhe,ckhe->chqk",
                queries[:, start_row:end_row],
                keys_all[:, :end_row],
                preferred_element_type=jnp.float32,
            )
            * scale
        )
        allowed = visible(drop_counts, lengths, start_row, QBLOCK, end_row)
        block_sums = jnp.transpose(log_sums[:, start_row:end_row], (0, 2, 1))[..., None]
        probs = jnp.where(
            allowed, jnp.exp(jnp.where(allowed, scores, masked_score) - block_sums), 0.0
        )
        grad_rows = grad_out[:, start_row:end_row]
        grad_probs = jnp.einsum(
            "cqhe,ckhe->chqk", grad_rows, values[:, :end_row], preferred_element_type=jnp.float32
        )
        centre = jnp.sum(probs * grad_probs, axis=-1, keepdims=True)
        grad_scores = (probs * (grad_probs - centre) * scale).astype(jnp.bfloat16)
        grad_query.append(
            jnp.einsum(
                "chqk,ckhe->cqhe",
                grad_scores,
                keys_all[:, :end_row],
                preferred_element_type=jnp.float32,
            ).astype(jnp.bfloat16)
        )
        grad_key = grad_key.at[:, :end_row].add(
            jnp.einsum(
                "chqk,cqhe->ckhe",
                grad_scores,
                queries[:, start_row:end_row],
                preferred_element_type=jnp.float32,
            )
        )
        grad_value = grad_value.at[:, :end_row].add(
            jnp.einsum(
                "chqk,cqhe->ckhe",
                probs.astype(jnp.bfloat16),
                grad_rows,
                preferred_element_type=jnp.float32,
            )
        )
    return jnp.stack(
        [
            jnp.concatenate(grad_query, axis=1),
            grad_key.astype(jnp.bfloat16),
            grad_value.astype(jnp.bfloat16),
        ],
        axis=3,
    )


def head_bias(pair_bias, head_count):
    stacked = jnp.stack([pair_bias[0], jnp.zeros_like(pair_bias[0]), pair_bias[1]]).astype(
        jnp.float32
    )
    return jnp.transpose(stacked.reshape(3, head_count, HD), (1, 0, 2))


def bias_grads(grad_packed):
    summed = jnp.sum(grad_packed, axis=(0, 1), dtype=jnp.float32)
    return jnp.stack([summed[:, 0].reshape(-1), summed[:, 2].reshape(-1)])


def body(
    cell_tokens,
    drop_counts,
    lengths,
    ln_gain,
    ln_shift,
    w_qkv,
    qv_bias,
    w_out,
    out_bias,
    w_up,
    up_bias,
    w_down,
    out_grad,
):
    scale = 1.0 / math.sqrt(HD)
    up_rows, down_rows = (
        lax.all_gather(w_up, "cells", axis=0, tiled=True),
        lax.all_gather(w_down, "cells", axis=0, tiled=True),
    )
    up_unit, down_unit = (
        lax.all_to_all(up_rows, "seq", split_axis=0, concat_axis=1, tiled=True),
        lax.all_to_all(down_rows, "seq", split_axis=0, concat_axis=1, tiled=True),
    )
    gains = ln_gain.astype(jnp.float32)
    shifts = ln_shift.astype(jnp.float32)
    biases = out_bias.astype(jnp.float32)
    tokens = cell_tokens.astype(jnp.float32)
    cells_here, rows_here, width = tokens.shape
    normed_f, norm_back = jax.vjp(layer_norm, tokens, gains[0], shifts[0])
    normed = normed_f.astype(jnp.bfloat16)
    qkv_full, out_full, bias_full = (
        lax.all_gather(w_qkv, "seq", axis=2, tiled=True),
        lax.all_gather(w_out, "seq", axis=0, tiled=True),
        lax.all_gather(qv_bias, "seq", axis=1, tiled=True),
    )
    qkv_heads = qkv_full.reshape(3, width, HEADS, HD)
    packed = jnp.einsum(
        "csd,tdhe->cshte", normed, qkv_heads, preferred_element_type=jnp.float32
    ) + head_bias(bias_full, HEADS)
    packed = packed.astype(jnp.bfloat16)
    group_count = lax.axis_size("seq")
    grouped = packed.reshape(cells_here, rows_here, group_count, HEADS // group_count, 3, HD)
    moved_heads = lax.all_to_all(grouped, "seq", split_axis=2, concat_axis=1, tiled=True)[:, :, 0]
    head_out, log_sums = attend(moved_heads, drop_counts, lengths, scale)
    head_out, log_sums, moved_kept = (head_out, log_sums, moved_heads)
    mixed = lax.all_to_all(head_out, "seq", split_axis=1, concat_axis=2, tiled=True).reshape(
        cells_here, rows_here, width
    )
    branch = (
        jnp.einsum("csd,de->cse", mixed, out_full, preferred_element_type=jnp.float32) + biases[0]
    )
    middle = tokens + branch
    normed2_f, norm_back2 = jax.vjp(layer_norm, middle, gains[1], shifts[1])
    normed2 = normed2_f.astype(jnp.bfloat16)
    normed2_all, grad_all = (
        lax.all_gather(normed2, "seq", axis=1, tiled=True),
        lax.all_gather(out_grad, "seq", axis=1, tiled=True),
    )
    units = up_unit.shape[0]
    first_unit = lax.axis_index("seq") * units
    bias_unit = lax.dynamic_slice_in_dim(up_bias, first_unit, units).astype(jnp.float32)
    hidden = (
        jnp.einsum("csd,fd->csf", normed2_all, up_unit, preferred_element_type=jnp.float32)
        + bias_unit
    )
    active_f, gelu_back = jax.vjp(gelu_tanh, hidden)
    active = active_f.astype(jnp.bfloat16)
    down_terms = jnp.einsum("csf,fd->csd", active, down_unit, preferred_element_type=jnp.float32)
    branch2 = (
        lax.psum_scatter(
            down_terms.astype(jnp.bfloat16), "seq", scatter_dimension=1, tiled=True
        ).astype(jnp.float32)
        + biases[1]
    )
    block_out = (middle + branch2).astype(jnp.bfloat16)
    grad_down_unit = jnp.einsum("csf,csd->fd", active, grad_all, preferred_element_type=jnp.float32)
    grad_active = jnp.einsum("csd,fd->csf", grad_all, down_unit, preferred_element_type=jnp.float32)
    grad_hidden = gelu_back(grad_active)[0].astype(jnp.bfloat16)
    grad_up_unit = jnp.einsum(
        "csf,csd->fd", grad_hidden, normed2_all, preferred_element_type=jnp.float32
    )
    unit_bias_grad = jnp.sum(grad_hidden, axis=(0, 1), dtype=jnp.float32)
    grad_up_bias = lax.dynamic_update_slice_in_dim(
        jnp.zeros((up_bias.shape[0],), jnp.float32), unit_bias_grad, first_unit, 0
    )
    normed2_terms = jnp.einsum(
        "csf,fd->csd", grad_hidden, up_unit, preferred_element_type=jnp.float32
    )
    grad_normed2 = lax.psum_scatter(normed2_terms, "seq", scatter_dimension=1, tiled=True)
    up_part, down_part = (
        lax.all_to_all(grad_up_unit, "seq", split_axis=1, concat_axis=0, tiled=True),
        lax.all_to_all(grad_down_unit, "seq", split_axis=1, concat_axis=0, tiled=True),
    )
    grad_middle_norm, grad_gain2, grad_shift2 = norm_back2(grad_normed2)
    grad_middle = out_grad.astype(jnp.float32) + grad_middle_norm
    grad_branch = grad_middle.astype(jnp.bfloat16)
    grad_bias_attn = jnp.sum(grad_branch, axis=(0, 1), dtype=jnp.float32)
    grad_bias_down = jnp.sum(out_grad, axis=(0, 1), dtype=jnp.float32)
    d_up, d_down = (
        lax.psum_scatter(up_part, "cells", scatter_dimension=0, tiled=True),
        lax.psum_scatter(down_part, "cells", scatter_dimension=0, tiled=True),
    )
    grad_out_w = jnp.einsum("csd,cse->de", mixed, grad_branch, preferred_element_type=jnp.float32)
    grad_mixed = jnp.einsum(
        "cse,de->csd", grad_branch, out_full, preferred_element_type=jnp.float32
    ).astype(jnp.bfloat16)
    grad_mixed = grad_mixed.reshape(cells_here, rows_here, HEADS, HD)
    grad_heads = lax.all_to_all(grad_mixed, "seq", split_axis=2, concat_axis=1, tiled=True)
    grad_packed_heads = attend_back(moved_kept, grad_heads, log_sums, drop_counts, lengths, scale)
    grad_packed = lax.all_to_all(grad_packed_heads, "seq", split_axis=1, concat_axis=2, tiled=True)
    grad_qkv_full = jnp.einsum(
        "csd,cshte->tdhe", normed, grad_packed, preferred_element_type=jnp.float32
    ).reshape(3, width, width)
    grad_normed = jnp.einsum(
        "cshte,tdhe->csd", grad_packed, qkv_heads, preferred_element_type=jnp.float32
    )
    grad_qkv_own, grad_bias_own, grad_out_own = (
        lax.psum_scatter(grad_qkv_full, "seq", scatter_dimension=2, tiled=True),
        lax.psum_scatter(bias_grads(grad_packed), "seq", scatter_dimension=1, tiled=True),
        lax.psum_scatter(grad_out_w, "seq", scatter_dimension=0, tiled=True),
    )
    d_qkv, d_qv_bias, d_out = lax.psum((grad_qkv_own, grad_bias_own, grad_out_own), "cells")
    grad_tokens_norm, grad_gain1, grad_shift1 = norm_back(grad_normed)
    in_grad = grad_middle + grad_tokens_norm
    d_ln_gain, d_ln_shift, d_out_bias, d_up_bias = lax.psum(
        (
            jnp.stack([grad_gain1, grad_gain2]),
            jnp.stack([grad_shift1, grad_shift2]),
            jnp.stack([grad_bias_attn, grad_bias_down]),
            grad_up_bias,
        ),
        ("cells", "seq"),
    )
    return (
        block_out,
        in_grad,
        d_ln_gain,
        d_ln_shift,
        d_qkv,
        d_qv_bias,
        d_out,
        d_out_bias,
        d_up,
        d_up_bias,
        d_down,
    )


def solution(mesh):
    placed = (
        P("cells", "seq", None),
        P("cells"),
        P("cells"),
        P(),
        P(),
        P(None, None, "seq"),
        P(None, "seq"),
        P("seq", None),
        P(),
        P("cells", "seq"),
        P(),
        P("cells", "seq"),
        P("cells", "seq", None),
    )
    return jax.shard_map(
        body,
        mesh=mesh,
        in_specs=placed,
        out_specs=(
            P("cells", "seq", None),
            P("cells", "seq", None),
            P(),
            P(),
            P(None, None, "seq"),
            P(None, "seq"),
            P("seq", None),
            P(),
            P("cells", "seq"),
            P(),
            P("cells", "seq"),
        ),
        check_vma=False,
    )
```

profile of v0, /device:TPU:0, one launch (start us, length us, event | category | flops | bytes accessed | tf_op | source)
XLA Modules:
  0.0 1321.3 jit_solution(9016403108067090573)
XLA Ops:
  21.2 45.7 %all-gather.10.cloned.1.call-done = bf16[3,1120,1120]{1,2,0:T(8,128)(2,1)} async-done(((bf16[3,1120,280]{1,2,0:T(8,128)(2,1)}), bf16[3,1120,1120]{1,2,0:T(8,128)(2,1)}) %all-gather.10.cloned.1.call-update) | async-done | bytes 7526416 | tf_op jit(solution)/shard_map/all_gather | solution.py:175
  84.5 35.4 %all-to-all-done = bf16[1,320,4,5,3,56]{1,5,3,4,0,2:T(8,128)(2,1)S(1)} async-done(((bf16[1,320,4,5,3,56]{1,5,3,4,0,2:T(8,128)(2,1)}), bf16[1,320,4,5,3,56]{1,5,3,4,0,2:T(8,128)(2,1)S(1)}, u32[]{:S(2)}, u32[]{:S(2)}) %all-to-all-start) | async-done | bytes 2150432 | tf_op jit(solution)/shard_map/all_to_all | solution.py:186
  127.1 9.1 fusion.181
  143.2 9.6 fusion.6
  152.9 9.2 fusion.122
  173.1 10.9 all-to-all-done.1
  234.2 25.9 %all-to-all-done.2 = bf16[4,1120,280]{1,2,0:T(8,128)(2,1)} async-done(((bf16[4,1120,280]{1,2,0:T(8,128)(2,1)}), bf16[4,1120,280]{1,2,0:T(8,128)(2,1)}, u32[]{:S(2)}, u32[]{:S(2)}) %all-to-all-start.2) | async-done | bytes 2508832 | tf_op jit(solution)/shard_map/all_to_all | solution.py:164
  265.5 9.1 convolution_add_fusion
  274.6 33.1 %all-gather.16.cloned.1.call-done = bf16[1,1280,1120]{2,1,0:T(8,128)(2,1)} async-done(((bf16[1,320,1120]{2,1,0:T(8,128)(2,1)}), bf16[1,1280,1120]{2,1,0:T(8,128)(2,1)}) %all-gather.16.cloned.1.call-update) | async-done | bytes 2867216 | tf_op jit(solution)/shard_map/all_gather | solution.py:200
  311.4 12.8 convert_reduce_fusion
  333.9 10.4 fusion.36
  344.4 45.2 %reduce-scatter.16.cloned.1.call-done = f32[1,320,1120]{2,1,0:T(8,128)} async-done(((f32[1,1280,1120]{2,1,0:T(8,128)}), f32[1,320,1120]{2,1,0:T(8,128)}) %reduce-scatter.16.cloned.1.call-update) | async-done | bytes 1433616 | tf_op jit(solution)/shard_map/reduce_scatter | solution.py:232
  391.5 38.1 %reduce-scatter.14.cloned.1.call-done = bf16[1,320,1120]{2,1,0:T(8,128)(2,1)} async-done(((bf16[1,1280,1120]{2,1,0:T(8,128)(2,1)}), bf16[1,320,1120]{2,1,0:T(8,128)(2,1)}) %reduce-scatter.14.cloned.1.call-update) | async-done | bytes 716816 | tf_op jit(solution)/shard_map/reduce_scatter | solution.py:213
  446.1 12.2 all-to-all-done.4
  465.0 17.3 %fusion.123 = bf16[1,640,5,56]{1,3,2,0:T(8,128)(2,1)} fusion(f32[5,640,640]{1,2,0:T(8,128)} %fusion.146, bf16[1,1280,5,56]{1,3,2,0:T(8,128)(2,1)S(1)} %copy-done.19, f32[5,640,640]{1,2,0:T(8,128)} %copy-done.7, f32[5,640]{1,0:T(8,128)S(1)} %log_add_fusion.1, pred[640,640]{0,1:T(8,128)(4,1)S(1)} %copy-done.14), kind=kOutput, calls=%fused_computation.124 | convolution fusion | flops 256183040 | bytes 34344960 | tf_op jit(solution)/shard_map/chqk,ckhe->cqhe/dot_general | solution.py:98
  482.3 17.6 %fusion.111 = f32[1,640,5,56]{1,3,2,0:T(8,128)} fusion(f32[5,640,640]{1,2,0:T(8,128)} %fusion.146, bf16[1,1280,5,56]{1,3,2,0:T(8,128)(2,1)} %copy-done.15, f32[5,640,640]{1,2,0:T(8,128)} %copy-done.7, f32[5,640]{1,0:T(8,128)S(1)} %log_add_fusion.1, pred[640,640]{0,1:T(8,128)(4,1)S(1)} %copy-done.14), kind=kOutput, calls=%fused_computation.118 | convolution fusion | flops 256003840 | bytes 34703360 | tf_op jit(solution)/shard_map/chqk,cqhe->ckhe/dot_general | solution.py:106
  499.9 9.0 fusion.139
  508.9 35.1 %fusion.91 = bf16[1,1280,5,1,56]{1,4,2,3,0:T(8,128)(2,1)} fusion(f32[5,640,1280]{2,1,0:T(8,128)} %fusion.139, f32[5,640,1280]{2,1,0:T(8,128)} %get-tuple-element.107, f32[5,640]{1,0:T(8,128)S(1)} %log_add_fusion, pred[640,1280]{1,0:T(8,128)(4,1)} %fusion.57, f32[1,640,5,56]{1,3,2,0:T(8,128)} %fusion.111, bf16[1,1280,5,56]{1,3,2,0:T(8,128)(2,1)} %copy-done.15), kind=kOutput, calls=%fused_computation.84 | convolution fusion | flops 496337280 | bytes 69007360 | tf_op jit(solution)/shard_map/chqk,cqhe->ckhe/dot_general | solution.py:106
  544.0 33.6 %fusion.127 = bf16[1,640,5,56]{1,3,2,0:T(8,128)(2,1)} fusion(f32[5,640,1280]{2,1,0:T(8,128)} %fusion.139, f32[5,640,1280]{2,1,0:T(8,128)} %get-tuple-element.107, f32[5,640]{1,0:T(8,128)S(1)} %log_add_fusion, pred[640,1280]{1,0:T(8,128)(4,1)} %fusion.57, bf16[1,1280,5,3,56]{1,4,2,3,0:T(8,128)(2,1)S(1)} %copy-done.2), kind=kOutput, calls=%fused_computation.126 | convolution fusion | flops 495799680 | bytes 68290560 | tf_op jit(solution)/shard_map/chqk,ckhe->cqhe/dot_general | solution.py:98
  584.9 8.4 fusion.88
  599.8 10.7 reshape.829
  610.5 29.5 %all_to_all.133 = bf16[4,2,134400]{2,1,0:T(2,128)(2,1)} all-to-all(bf16[4,2,134400]{2,1,0:T(2,128)(2,1)S(1)} %reshape.829), channel_id=1, replica_groups=mesh['cells'=8,'seq'=4] {'seq'}, dimensions={0} | all-to-all | bytes 4300800 | tf_op jit(solution)/shard_map/all_to_all | solution.py:253
  640.1 12.7 reshape.830
  652.8 11.0 copy.105
  674.0 11.8 copy.108
  691.4 8.5 fusion.64
  700.0 104.3 %all_to_all.134 = f32[1120,4,280]{0,2,1:T(8,128)} all-to-all(f32[1120,4,280]{0,2,1:T(8,128)S(1)} %fusion.64), channel_id=1, replica_groups=mesh['cells'=8,'seq'=4] {'seq'}, dimensions={1} | all-to-all | bytes 10035200 | tf_op jit(solution)/shard_map/all_to_all | solution.py:235
  823.3 77.0 %all_to_all.135 = f32[1120,4,280]{0,2,1:T(8,128)} all-to-all(f32[1120,4,280]{0,2,1:T(8,128)S(1)} %fusion.66), channel_id=1, replica_groups=mesh['cells'=8,'seq'=4] {'seq'}, dimensions={1} | all-to-all | bytes 10035200 | tf_op jit(solution)/shard_map/all_to_all | solution.py:234
  929.9 22.3 %psum.52 = f32[2,280]{1,0:T(2,128)} all-reduce(f32[2,280]{1,0:T(2,128)S(1)} %constant_dynamic-slice_fusion), channel_id=1, replica_groups=mesh['cells'=8,'seq'=4] {'cells'}, use_global_device_ids=true, to_apply=%region_26.27 | all-reduce | flops 560 | bytes 4480 | tf_op jit(solution)/shard_map/psum | solution.py:265
  952.2 41.3 %all-reduce.4 = (f32[2,1120]{1,0:T(2,128)}, f32[2,1120]{1,0:T(2,128)}, f32[2,1120]{1,0:T(2,128)}, f32[4480]{0:T(1024)}) all-reduce(f32[2,1120]{1,0:T(2,128)S(1)} %pad_maximum_fusion.2, f32[2,1120]{1,0:T(2,128)S(1)} %pad_maximum_fusion.3, f32[2,1120]{1,0:T(2,128)S(1)} %pad_maximum_fusion.5, ...), channel_id=1, replica_groups=mesh['cells'=8,'seq'=4] {'cells','seq'}, use_global_device_ids=true, to_apply=%region_18.19 | all-reduce | flops 11200 | bytes 89600 | tf_op jit(solution)/shard_map/psum | solution.py:268
  996.4 127.5 %reduce-scatter.20.cloned.1.call-done = f32[560,280]{1,0:T(8,128)} async-done(((f32[4480,280]{1,0:T(8,128)}), f32[560,280]{1,0:T(8,128)}) %reduce-scatter.20.cloned.1.call-update) | async-done | bytes 627216
  1126.2 183.0 %all-reduce.8.cloned.1.call-done = (f32[3,1120,280]{1,2,0:T(8,128)}, f32[280,1120]{1,0:T(8,128)}) async-done(((f32[3,1120,280]{1,2,0:T(8,128)}, f32[280,1120]{1,0:T(8,128)}), (f32[3,1120,280]{1,2,0:T(8,128)}, f32[280,1120]{1,0:T(8,128)})) %all-reduce.8.cloned.1.call-update) | async-done | bytes 5017616 | tf_op jit(solution)/shard_map/psum | solution.py:265
  (213 shorter events, 237.1 us)
Async XLA Ops:
  7.2 59.7 %all-gather.10.cloned.1.call-start = ((), (), s32[]{:S(2)}) async-start(), calls=%async_computation.14 | async-start | bytes 9676800 | tf_op jit(solution)/shard_map/all_gather | solution.py:175
  7.9 183.1 %all-gather.12.cloned.1.call-start = ((), (), s32[]{:S(2)}) async-start(), calls=%async_computation.15 | async-start | bytes 3225600 | tf_op jit(solution)/shard_map/all_gather | solution.py:176
  8.7 188.3 %all-gather.18.cloned.1.call-start = ((), (), s32[]{:S(2)}) async-start(), calls=%async_computation.21 | async-start | bytes 3225600 | tf_op jit(solution)/shard_map/all_gather | solution.py:160
  17.5 56.8 %copy-start.21 = (f32[1120]{0:T(1024)}, f32[1120]{0:T(1024)S(1)}, u32[]{:S(2)}) copy-start(f32[1120]{0:T(1024)S(1)} %get-tuple-element.85) | copy-start | bytes 13444
  17.6 56.8 %copy-start.27 = (f32[1120]{0:T(1024)}, f32[1120]{0:T(1024)S(1)}, u32[]{:S(2)}) copy-start(f32[1120]{0:T(1024)S(1)} %get-tuple-element.87) | copy-start | bytes 13444
  19.0 55.4 %copy-start.23 = (f32[320]{0:T(512)}, f32[320]{0:T(512)S(1)}, u32[]{:S(2)}) copy-start(f32[320]{0:T(512)S(1)} %broadcast_multiply_fusion.1) | copy-start | bytes 3844
  21.2 53.2 %copy-start.25 = (f32[320]{0:T(512)}, f32[320]{0:T(512)S(1)}, u32[]{:S(2)}) copy-start(f32[320]{0:T(512)S(1)} %fusion.148) | copy-start | bytes 3844
  76.8 43.2 %all-to-all-start = ((bf16[1,320,4,5,3,56]{1,5,3,4,0,2:T(8,128)(2,1)}), bf16[1,320,4,5,3,56]{1,5,3,4,0,2:T(8,128)(2,1)S(1)}, u32[]{:S(2)}, u32[]{:S(2)}) async-start(bf16[1,320,4,5,3,56]{1,5,3,4,0,2:T(8,128)(2,1)} %copy.87), calls=%async_computation | async-start | bytes 5160960 | tf_op jit(solution)/shard_map/all_to_all | solution.py:186
  80.4 140.4 %all-gather.20.cloned.1.call-start = ((), (), s32[]{:S(2)}) async-start(), calls=%async_computation.22 | async-start | bytes 3225600 | tf_op jit(solution)/shard_map/all_gather | solution.py:161
  82.6 57.8 %copy-start.13 = (pred[640,640]{0,1:T(8,128)(4,1)}, pred[640,640]{0,1:T(8,128)(4,1)S(1)}, u32[]{:S(2)}) copy-start(pred[640,640]{0,1:T(8,128)(4,1)S(1)} %fusion.101) | copy-start | bytes 1228804
  126.9 26.0 %copy-start.1 = (bf16[1,1280,5,3,56]{1,4,2,3,0:T(8,128)(2,1)}, bf16[1,1280,5,3,56]{1,4,2,3,0:T(8,128)(2,1)S(1)}, u32[]{:S(2)}) copy-start(bf16[1,1280,5,3,56]{1,4,2,3,0:T(8,128)(2,1)S(1)} %squeeze.15) | copy-start | bytes 6451204
  127.1 13.4 %copy-start.16 = (bf16[1,1280,5,56]{1,3,2,0:T(8,128)(2,1)}, bf16[1,1280,5,56]{1,3,2,0:T(8,128)(2,1)S(1)}, u32[]{:S(2)}) copy-start(bf16[1,1280,5,56]{1,3,2,0:T(8,128)(2,1)S(1)} %get-tuple-element.100) | copy-start | bytes 2150404
  165.0 26.0 %copy-start = (bf16[1,320,1120]{2,1,0:T(8,128)(2,1)S(1)}, bf16[1,320,1120]{2,1,0:T(8,128)(2,1)}, u32[]{:S(2)}) copy-start(bf16[1,320,1120]{2,1,0:T(8,128)(2,1)} %param.25) | copy-start | bytes 2150404
  168.8 15.2 %all-to-all-start.1 = ((bf16[4,2,44800]{2,1,0:T(2,128)(2,1)}), bf16[4,2,44800]{2,1,0:T(2,128)(2,1)}, u32[]{:S(2)}, u32[]{:S(2)}) async-start(bf16[4,2,44800]{2,1,0:T(2,128)(2,1)} %reshape.827), calls=%async_computation.1 | async-start | bytes 1433600 | tf_op jit(solution)/shard_map/all_to_all | solution.py:189
  173.0 92.5 %all-gather.14.cloned.1.call-start = ((), (), s32[]{:S(2)}) async-start(), calls=%async_computation.16 | async-start | bytes 3686400 | tf_op jit(solution)/shard_map/all_gather | solution.py:199
  196.3 111.3 %all-gather.16.cloned.1.call-start = ((), (), s32[]{:S(2)}) async-start(), calls=%async_computation.18 | async-start | bytes 3686400 | tf_op jit(solution)/shard_map/all_gather | solution.py:200
  210.2 49.9 %all-to-all-start.2 = ((bf16[4,1120,280]{1,2,0:T(8,128)(2,1)}), bf16[4,1120,280]{1,2,0:T(8,128)(2,1)}, u32[]{:S(2)}, u32[]{:S(2)}) async-start(bf16[4,1120,280]{1,2,0:T(8,128)(2,1)} %copy.93), calls=%async_computation.2 | async-start | bytes 5160960 | tf_op jit(solution)/shard_map/all_to_all | solution.py:164
  260.1 51.3 %all-to-all-start.3 = ((bf16[4,1120,280]{1,2,0:T(8,128)(2,1)}), bf16[4,1120,280]{1,2,0:T(8,128)(2,1)}, u32[]{:S(2)}, u32[]{:S(2)}) async-start(bf16[4,1120,280]{1,2,0:T(8,128)(2,1)} %copy.95), calls=%async_computation.3 | async-start | bytes 5160960 | tf_op jit(solution)/shard_map/all_to_all | solution.py:165
  264.7 124.9 %reduce-scatter.16.cloned.1.call-start = ((), (), s32[]{:S(2)}) async-start(), calls=%async_computation.19 | async-start | bytes 7372800 | tf_op jit(solution)/shard_map/reduce_scatter | solution.py:232
  333.9 95.8 %reduce-scatter.14.cloned.1.call-start = ((), (), s32[]{:S(2)}) async-start(), calls=%async_computation.17 | async-start | bytes 3686400 | tf_op jit(solution)/shard_map/reduce_scatter | solution.py:213
  344.4 562.7 %reduce-scatter.24.cloned.1.call-start = ((), (), s32[]{:S(2)}) async-start(), calls=%async_computation.25 | async-start | bytes 6451200
  391.5 42.6 %copy-start.6 = (bf16[1,4,320,5,56]{2,4,3,1,0:T(8,128)(2,1)S(1)}, bf16[1,4,320,5,56]{2,4,3,1,0:T(8,128)(2,1)}, u32[]{:S(2)}) copy-start(bf16[1,4,320,5,56]{2,4,3,1,0:T(8,128)(2,1)} %copy.91) | copy-start | bytes 2150404
  442.3 15.9 %all-to-all-start.4 = ((bf16[1,320,20,56]{1,3,0,2:T(8,128)(2,1)}), bf16[1,320,20,56]{1,3,0,2:T(8,128)(2,1)S(1)}, u32[]{:S(2)}, u32[]{:S(2)}) async-start(bf16[1,320,20,56]{1,3,0,2:T(8,128)(2,1)} %bitcast.48), calls=%async_computation.6 | async-start | bytes 1720320 | tf_op jit(solution)/shard_map/all_to_all | solution.py:251
  445.8 461.2 %reduce-scatter.18.cloned.1.call-start = ((), (), s32[]{:S(2)}) async-start(), calls=%async_computation.20 | async-start | bytes 19353600 | tf_op jit(solution)/shard_map/reduce_scatter | solution.py:261
  482.3 17.6 %copy-start.2 = (bf16[1,1280,5,3,56]{1,4,2,3,0:T(8,128)(2,1)S(1)}, bf16[1,1280,5,3,56]{1,4,2,3,0:T(8,128)(2,1)}, u32[]{:S(2)}) copy-start(bf16[1,1280,5,3,56]{1,4,2,3,0:T(8,128)(2,1)} %copy-done.1) | copy-start | bytes 6451204
  652.8 12.8 copy-start.22
  652.8 12.8 copy-start.24
  652.8 12.8 copy-start.26
  652.8 12.8 copy-start.28
  685.8 308.2 %reduce-scatter.22.cloned.1.call-start = ((), (), s32[]{:S(2)}) async-start(), calls=%async_computation.24 | async-start | bytes 7741440
  811.2 312.7 %reduce-scatter.20.cloned.1.call-start = ((), (), s32[]{:S(2)}) async-start(), calls=%async_computation.23 | async-start | bytes 7741440
  907.0 402.2 %all-reduce.8.cloned.1.call-start = ((), (), s32[]{:S(2)}) async-start(), calls=%async_computation.26 | async-start | bytes 10321920 | tf_op jit(solution)/shard_map/psum | solution.py:265
  (21 other events, 113.8 us)
Sparse Core Ops, SparseCore 0:
  9.6 57.3 all-gather.9
  68.5 34.0 all-gather.11
  104.8 57.7 all-gather.17
  164.7 56.1 all-gather.19
  222.8 40.0 all-gather.13
  264.4 43.2 all-gather.15
  334.0 55.5 reduce-scatter.15
  392.9 36.7 reduce-scatter.13
  438.1 50.8 reduce-scatter.23
  686.0 175.8 reduce-scatter.17
  865.9 128.0 reduce-scatter.21
  998.0 125.7 reduce-scatter.19
  1128.0 181.1 all-reduce.7
where the time goes:
time: 1330 us; the launch traced here: 1320 us
  waiting for transfers between devices  571 us (43%)
  blocking collectives  287 us (22%)
  matrix products  245 us (18%)
  local copies, waits for them, and re-layouts  147 us (11%)
  other arithmetic  33.3 us (3%)
  starting transfers between devices  21.5 us (2%)
  between operations  16.9 us (1%)
    psum x1, waiting for transfers between devices, body(): lax.psum((grad_qkv_own, grad_bias_own, grad_out_own), 'cells')  183 us
    unnamed x16, waiting for transfers between devices  132 us
    all_to_all x1, blocking collectives, body(): lax.all_to_all(grad_down_unit, 'seq', split_axis=1, concat_axis=0, tiled=...  104 us
    all_to_all x1, blocking collectives, body(): lax.all_to_all(grad_up_unit, 'seq', split_axis=1, concat_axis=0, tiled=True)  77 us
    unnamed x83, local copies, waits for them, and re-layouts  60.8 us
    dot_general x2, matrix products, attend_back(): jnp.einsum('chqk,cqhe->ckhe', grad_scores, queries[:, start_row:end_row],...  52.7 us
    dot_general x2, matrix products, attend_back(): jnp.einsum('chqk,ckhe->cqhe', grad_scores, keys_all[:, :end_row], preferr...  50.9 us
    all_gather x1, waiting for transfers between devices, body(): lax.all_gather(w_qkv, 'seq', axis=2, tiled=True)  45.7 us
  transfers between devices with their start and end apart: 18, of which 13 were waited for; matrix products, arithmetic and copies ran while one was open for 28% of the time, Pallas kernels for 0%

commit v1 on v0

--- a/solution.py
+++ b/solution.py
@@ -9,6 +9,22 @@
 QBLOCK = 640
 epsilon = 1e-05
 masked_score = -1e30
+
+
+def ring_gather(x, axis, dim):
+    ways, here, turn = (lax.axis_size(axis), lax.axis_index(axis), x.shape[dim])
+    lengths = [n * ways if d == dim else n for d, n in enumerate(x.shape)]
+    full = lax.dynamic_update_slice_in_dim(jnp.zeros(lengths, x.dtype), x, here * turn, axis=dim)
+    going_up = going_down = x
+    for far in range(1, ways // 2 + 1):
+        going_up = lax.ppermute(going_up, axis, [(d, (d + 1) % ways) for d in range(ways)])
+        full = lax.dynamic_update_slice_in_dim(full, going_up, (here - far) % ways * turn, axis=dim)
+        if 2 * far < ways:
+            going_down = lax.ppermute(going_down, axis, [(d, (d - 1) % ways) for d in range(ways)])
+            full = lax.dynamic_update_slice_in_dim(
+                full, going_down, (here + far) % ways * turn, axis=dim
+            )
+    return full
 
 
 def layer_norm(rows, gain, shift):
@@ -197,7 +213,7 @@
     normed2 = normed2_f.astype(jnp.bfloat16)
     normed2_all, grad_all = (
         lax.all_gather(normed2, "seq", axis=1, tiled=True),
-        lax.all_gather(out_grad, "seq", axis=1, tiled=True),
+        ring_gather(out_grad, "seq", 1),
     )
     units = up_unit.shape[0]
     first_unit = lax.axis_index("seq") * units

time: 1330 us -> 1370 us (1.030)
  local copies, waits for them, and re-layouts: 147 us -> 189 us
    dynamic_update_slice x0 -> x4, local copies, waits for them, and re-layouts: none -> 37.5 us  [the longest x2 18.4 us: ring_gather(): lax.dynamic_update_slice_in_dim(full, going_up, (here - far) % ways * tur...]
    all_gather x1 -> x0, waiting for transfers between devices: 33.1 us -> none  [body(): lax.all_gather(out_grad, 'seq', axis=1, tiled=True)]
    ppermute x0 -> x3, waiting for transfers between devices: none -> 29.8 us  [the longest x1 26 us: ring_gather(): lax.ppermute(going_down, axis, [(d, (d - 1) % ways) for d in range(ways)])]
    unnamed x16 -> x15, waiting for transfers between devices: 132 us -> 138 us
    unnamed x83 -> x85, local copies, waits for them, and re-layouts: 60.8 us -> 60.5 us
  transfers between devices with their start and end apart: 18 -> 20, of which waited for: 13 -> 13; matrix products, arithmetic and copies ran while one was open for 28% -> 30% of each run, Pallas kernels for 0% -> 0%
where the time goes in v1:
time: 1370 us; the launch traced here: 1360 us
  waiting for transfers between devices  571 us (42%)
  blocking collectives  286 us (21%)
  matrix products  244 us (18%)
  local copies, waits for them, and re-layouts  189 us (14%)
  other arithmetic  33.3 us (2%)
  starting transfers between devices  24 us (2%)
  between operations  17.2 us (1%)
    psum x1, waiting for transfers between devices, body(): lax.psum((grad_qkv_own, grad_bias_own, grad_out_own), 'cells')  183 us
    unnamed x15, waiting for transfers between devices  138 us
    all_to_all x1, blocking collectives, body(): lax.all_to_all(grad_down_unit, 'seq', split_axis=1, concat_axis=0, tiled=...  98.1 us
    all_to_all x1, blocking collectives, body(): lax.all_to_all(grad_up_unit, 'seq', split_axis=1, concat_axis=0, tiled=True)  83.3 us
    unnamed x85, local copies, waits for them, and re-layouts  60.5 us
    dot_general x2, matrix products, attend_back(): jnp.einsum('chqk,cqhe->ckhe', grad_scores, queries[:, start_row:end_row],...  52.7 us
    dot_general x2, matrix products, attend_back(): jnp.einsum('chqk,ckhe->cqhe', grad_scores, keys_all[:, :end_row], preferr...  50.9 us
    reduce_scatter x1, waiting for transfers between devices, body(): lax.psum_scatter(normed2_terms, 'seq', scatter_dimension=1, tiled=True)  46.2 us
  transfers between devices with their start and end apart: 20, of which 13 were waited for; matrix products, arithmetic and copies ran while one was open for 30% of the time, Pallas kernels for 0%

profile of v1, /device:TPU:0, one launch (start us, length us, event | category | flops | bytes accessed | tf_op | source)
XLA Modules:
  0.0 1364.1 jit_solution(8395270514615228451)
XLA Ops:
  21.3 45.7 %all-gather.9.cloned.1.call-done = bf16[3,1120,1120]{1,2,0:T(8,128)(2,1)} async-done(((bf16[3,1120,280]{1,2,0:T(8,128)(2,1)}), bf16[3,1120,1120]{1,2,0:T(8,128)(2,1)}) %all-gather.9.cloned.1.call-update) | async-done | bytes 7526416 | tf_op jit(solution)/shard_map/all_gather | solution.py:191
  84.5 35.4 %all-to-all-done = bf16[1,320,4,5,3,56]{1,5,3,4,0,2:T(8,128)(2,1)S(1)} async-done(((bf16[1,320,4,5,3,56]{1,5,3,4,0,2:T(8,128)(2,1)}), bf16[1,320,4,5,3,56]{1,5,3,4,0,2:T(8,128)(2,1)S(1)}, u32[]{:S(2)}, u32[]{:S(2)}) %all-to-all-start) | async-done | bytes 2150432 | tf_op jit(solution)/shard_map/all_to_all | solution.py:202
  127.1 9.1 fusion.178
  143.2 9.6 fusion.6
  152.9 9.1 fusion.118
  173.1 10.9 all-to-all-done.1
  234.2 25.4 %all-to-all-done.2 = bf16[4,1120,280]{1,2,0:T(8,128)(2,1)} async-done(((bf16[4,1120,280]{1,2,0:T(8,128)(2,1)}), bf16[4,1120,280]{1,2,0:T(8,128)(2,1)}, u32[]{:S(2)}, u32[]{:S(2)}) %all-to-all-start.2) | async-done | bytes 2508832 | tf_op jit(solution)/shard_map/all_to_all | solution.py:180
  273.0 9.2 dynamic_update_slice.19
  283.0 26.0 %collective-permute-done.1 = bf16[1,320,1120]{2,1,0:T(8,128)(2,1)} collective-permute-done((bf16[1,320,1120]{2,1,0:T(8,128)(2,1)S(1)}, bf16[1,320,1120]{2,1,0:T(8,128)(2,1)}, u32[]{:S(2)}, u32[]{:S(2)}) %collective-permute-start.1) | collective-permute-done | bytes 716832 | tf_op jit(solution)/shard_map/ppermute | solution.py:23
  313.4 9.6 dynamic_update_slice.20
  323.1 9.9 dynamic_update_slice.21
  344.1 9.1 convolution_add_fusion
  353.1 12.0 convert_reduce_fusion
  375.3 10.8 fusion.36
  386.1 46.2 %reduce-scatter.16.cloned.1.call-done = f32[1,320,1120]{2,1,0:T(8,128)} async-done(((f32[1,1280,1120]{2,1,0:T(8,128)}), f32[1,320,1120]{2,1,0:T(8,128)}) %reduce-scatter.16.cloned.1.call-update) | async-done | bytes 1433616 | tf_op jit(solution)/shard_map/reduce_scatter | solution.py:248
  434.3 38.1 %reduce-scatter.14.cloned.1.call-done = bf16[1,320,1120]{2,1,0:T(8,128)(2,1)} async-done(((bf16[1,1280,1120]{2,1,0:T(8,128)(2,1)}), bf16[1,320,1120]{2,1,0:T(8,128)(2,1)}) %reduce-scatter.14.cloned.1.call-update) | async-done | bytes 716816 | tf_op jit(solution)/shard_map/reduce_scatter | solution.py:229
  488.9 12.2 all-to-all-done.4
  507.8 17.3 %fusion.119 = bf16[1,640,5,56]{1,3,2,0:T(8,128)(2,1)} fusion(f32[5,640,640]{1,2,0:T(8,128)} %fusion.142, bf16[1,1280,5,56]{1,3,2,0:T(8,128)(2,1)S(1)} %copy-done.20, f32[5,640,640]{1,2,0:T(8,128)} %copy-done.7, f32[5,640]{1,0:T(8,128)S(1)} %log_add_fusion.1, pred[640,640]{0,1:T(8,128)(4,1)S(1)} %copy-done.15), kind=kOutput, calls=%fused_computation.122 | convolution fusion | flops 256183040 | bytes 34344960 | tf_op jit(solution)/shard_map/chqk,ckhe->cqhe/dot_general | solution.py:114
  525.1 17.6 %fusion.107 = f32[1,640,5,56]{1,3,2,0:T(8,128)} fusion(f32[5,640,640]{1,2,0:T(8,128)} %fusion.142, bf16[1,1280,5,56]{1,3,2,0:T(8,128)(2,1)} %copy-done.16, f32[5,640,640]{1,2,0:T(8,128)} %copy-done.7, f32[5,640]{1,0:T(8,128)S(1)} %log_add_fusion.1, pred[640,640]{0,1:T(8,128)(4,1)S(1)} %copy-done.15), kind=kOutput, calls=%fused_computation.116 | convolution fusion | flops 256003840 | bytes 34703360 | tf_op jit(solution)/shard_map/chqk,cqhe->ckhe/dot_general | solution.py:122
  551.7 35.0 %fusion.87 = bf16[1,1280,5,1,56]{1,4,2,3,0:T(8,128)(2,1)} fusion(f32[5,640,1280]{2,1,0:T(8,128)} %fusion.135, f32[5,640,1280]{2,1,0:T(8,128)} %get-tuple-element.109, f32[5,640]{1,0:T(8,128)S(1)} %log_add_fusion, pred[640,1280]{1,0:T(8,128)(4,1)} %fusion.57, f32[1,640,5,56]{1,3,2,0:T(8,128)} %fusion.107, bf16[1,1280,5,56]{1,3,2,0:T(8,128)(2,1)} %copy-done.16), kind=kOutput, calls=%fused_computation.82 | convolution fusion | flops 496337280 | bytes 69007360 | tf_op jit(solution)/shard_map/chqk,cqhe->ckhe/dot_general | solution.py:122
  586.8 33.6 %fusion.123 = bf16[1,640,5,56]{1,3,2,0:T(8,128)(2,1)} fusion(f32[5,640,1280]{2,1,0:T(8,128)} %fusion.135, f32[5,640,1280]{2,1,0:T(8,128)} %get-tuple-element.109, f32[5,640]{1,0:T(8,128)S(1)} %log_add_fusion, pred[640,1280]{1,0:T(8,128)(4,1)} %fusion.57, bf16[1,1280,5,3,56]{1,4,2,3,0:T(8,128)(2,1)S(1)} %copy-done.2), kind=kOutput, calls=%fused_computation.124 | convolution fusion | flops 495799680 | bytes 68290560 | tf_op jit(solution)/shard_map/chqk,ckhe->cqhe/dot_general | solution.py:114
  642.5 10.7 reshape.846
  653.2 29.5 %all_to_all.133 = bf16[4,2,134400]{2,1,0:T(2,128)(2,1)} all-to-all(bf16[4,2,134400]{2,1,0:T(2,128)(2,1)S(1)} %reshape.846), channel_id=1, replica_groups=mesh['cells'=8,'seq'=4] {'seq'}, dimensions={0} | all-to-all | bytes 4300800 | tf_op jit(solution)/shard_map/all_to_all | solution.py:269
  682.8 12.7 reshape.847
  695.5 11.0 copy.122
  716.7 11.8 copy.125
  736.3 98.1 %all_to_all.134 = f32[1120,4,280]{0,2,1:T(8,128)} all-to-all(f32[1120,4,280]{0,2,1:T(8,128)S(1)} %fusion.60), channel_id=1, replica_groups=mesh['cells'=8,'seq'=4] {'seq'}, dimensions={1} | all-to-all | bytes 10035200 | tf_op jit(solution)/shard_map/all_to_all | solution.py:251
  853.3 83.3 %all_to_all.135 = f32[1120,4,280]{0,2,1:T(8,128)} all-to-all(f32[1120,4,280]{0,2,1:T(8,128)S(1)} %fusion.62), channel_id=1, replica_groups=mesh['cells'=8,'seq'=4] {'seq'}, dimensions={1} | all-to-all | bytes 10035200 | tf_op jit(solution)/shard_map/all_to_all | solution.py:250
  965.8 22.2 %psum.52 = f32[2,280]{1,0:T(2,128)} all-reduce(f32[2,280]{1,0:T(2,128)S(1)} %constant_dynamic-slice_fusion), channel_id=1, replica_groups=mesh['cells'=8,'seq'=4] {'cells'}, use_global_device_ids=true, to_apply=%region_26.27 | all-reduce | flops 560 | bytes 4480 | tf_op jit(solution)/shard_map/psum | solution.py:281
  988.0 40.5 %all-reduce.4 = (f32[2,1120]{1,0:T(2,128)}, f32[2,1120]{1,0:T(2,128)}, f32[2,1120]{1,0:T(2,128)}, f32[4480]{0:T(1024)}) all-reduce(f32[2,1120]{1,0:T(2,128)S(1)} %pad_maximum_fusion.2, f32[2,1120]{1,0:T(2,128)S(1)} %pad_maximum_fusion.3, f32[2,1120]{1,0:T(2,128)S(1)} %pad_maximum_fusion.5, ...), channel_id=1, replica_groups=mesh['cells'=8,'seq'=4] {'cells','seq'}, use_global_device_ids=true, to_apply=%region_18.19 | all-reduce | flops 11200 | bytes 89600 | tf_op jit(solution)/shard_map/psum | solution.py:284
  1039.0 127.4 %reduce-scatter.20.cloned.1.call-done = f32[560,280]{1,0:T(8,128)} async-done(((f32[4480,280]{1,0:T(8,128)}), f32[560,280]{1,0:T(8,128)}) %reduce-scatter.20.cloned.1.call-update) | async-done | bytes 627216
  1168.8 182.9 %all-reduce.8.cloned.1.call-done = (f32[3,1120,280]{1,2,0:T(8,128)}, f32[280,1120]{1,0:T(8,128)}) async-done(((f32[3,1120,280]{1,2,0:T(8,128)}, f32[280,1120]{1,0:T(8,128)}), (f32[3,1120,280]{1,2,0:T(8,128)}, f32[280,1120]{1,0:T(8,128)})) %all-reduce.8.cloned.1.call-update) | async-done | bytes 5017616 | tf_op jit(solution)/shard_map/psum | solution.py:281
  (226 shorter events, 284.8 us)
Async XLA Ops:
  7.2 59.7 %all-gather.9.cloned.1.call-start = ((), (), s32[]{:S(2)}) async-start(), calls=%async_computation.14 | async-start | bytes 9676800 | tf_op jit(solution)/shard_map/all_gather | solution.py:191
  7.9 183.1 %all-gather.11.cloned.1.call-start = ((), (), s32[]{:S(2)}) async-start(), calls=%async_computation.15 | async-start | bytes 3225600 | tf_op jit(solution)/shard_map/all_gather | solution.py:192
  8.7 187.6 %all-gather.15.cloned.1.call-start = ((), (), s32[]{:S(2)}) async-start(), calls=%async_computation.20 | async-start | bytes 3225600 | tf_op jit(solution)/shard_map/all_gather | solution.py:176
  17.5 56.8 %copy-start.22 = (f32[1120]{0:T(1024)}, f32[1120]{0:T(1024)S(1)}, u32[]{:S(2)}) copy-start(f32[1120]{0:T(1024)S(1)} %get-tuple-element.85) | copy-start | bytes 13444
  17.6 56.8 %copy-start.28 = (f32[1120]{0:T(1024)}, f32[1120]{0:T(1024)S(1)}, u32[]{:S(2)}) copy-start(f32[1120]{0:T(1024)S(1)} %get-tuple-element.87) | copy-start | bytes 13444
  19.0 55.4 %copy-start.24 = (f32[320]{0:T(512)}, f32[320]{0:T(512)S(1)}, u32[]{:S(2)}) copy-start(f32[320]{0:T(512)S(1)} %broadcast_multiply_fusion.1) | copy-start | bytes 3844
  21.2 53.2 %copy-start.26 = (f32[320]{0:T(512)}, f32[320]{0:T(512)S(1)}, u32[]{:S(2)}) copy-start(f32[320]{0:T(512)S(1)} %fusion.144) | copy-start | bytes 3844
  76.8 43.2 %all-to-all-start = ((bf16[1,320,4,5,3,56]{1,5,3,4,0,2:T(8,128)(2,1)}), bf16[1,320,4,5,3,56]{1,5,3,4,0,2:T(8,128)(2,1)S(1)}, u32[]{:S(2)}, u32[]{:S(2)}) async-start(bf16[1,320,4,5,3,56]{1,5,3,4,0,2:T(8,128)(2,1)} %copy.99), calls=%async_computation | async-start | bytes 5160960 | tf_op jit(solution)/shard_map/all_to_all | solution.py:202
  80.4 140.4 %all-gather.17.cloned.1.call-start = ((), (), s32[]{:S(2)}) async-start(), calls=%async_computation.21 | async-start | bytes 3225600 | tf_op jit(solution)/shard_map/all_gather | solution.py:177
  82.6 57.8 %copy-start.14 = (pred[640,640]{0,1:T(8,128)(4,1)}, pred[640,640]{0,1:T(8,128)(4,1)S(1)}, u32[]{:S(2)}) copy-start(pred[640,640]{0,1:T(8,128)(4,1)S(1)} %fusion.97) | copy-start | bytes 1228804
  126.9 26.0 %copy-start.1 = (bf16[1,1280,5,3,56]{1,4,2,3,0:T(8,128)(2,1)}, bf16[1,1280,5,3,56]{1,4,2,3,0:T(8,128)(2,1)S(1)}, u32[]{:S(2)}) copy-start(bf16[1,1280,5,3,56]{1,4,2,3,0:T(8,128)(2,1)S(1)} %squeeze.15) | copy-start | bytes 6451204
  127.1 13.4 copy-start.17
  165.0 26.0 %copy-start = (bf16[1,320,1120]{2,1,0:T(8,128)(2,1)S(1)}, bf16[1,320,1120]{2,1,0:T(8,128)(2,1)}, u32[]{:S(2)}) copy-start(bf16[1,320,1120]{2,1,0:T(8,128)(2,1)} %param.25) | copy-start | bytes 2150404
  168.8 15.2 %all-to-all-start.1 = ((bf16[4,2,44800]{2,1,0:T(2,128)(2,1)}), bf16[4,2,44800]{2,1,0:T(2,128)(2,1)}, u32[]{:S(2)}, u32[]{:S(2)}) async-start(bf16[4,2,44800]{2,1,0:T(2,128)(2,1)} %reshape.844), calls=%async_computation.1 | async-start | bytes 1433600 | tf_op jit(solution)/shard_map/all_to_all | solution.py:205
  173.0 171.1 %all-gather.13.cloned.1.call-start = ((), (), s32[]{:S(2)}) async-start(), calls=%async_computation.16 | async-start | bytes 3686400 | tf_op jit(solution)/shard_map/all_gather | solution.py:215
  209.7 49.9 %all-to-all-start.2 = ((bf16[4,1120,280]{1,2,0:T(8,128)(2,1)}), bf16[4,1120,280]{1,2,0:T(8,128)(2,1)}, u32[]{:S(2)}, u32[]{:S(2)}) async-start(bf16[4,1120,280]{1,2,0:T(8,128)(2,1)} %copy.105), calls=%async_computation.2 | async-start | bytes 5160960 | tf_op jit(solution)/shard_map/all_to_all | solution.py:180
  214.3 55.5 %collective-permute-start = (bf16[1,320,1120]{2,1,0:T(8,128)(2,1)S(1)}, bf16[1,320,1120]{2,1,0:T(8,128)(2,1)}, u32[]{:S(2)}, u32[]{:S(2)}) collective-permute-start(bf16[1,320,1120]{2,1,0:T(8,128)(2,1)S(1)} %copy-done.9), channel_id=1, source_target_pairs={{0,1},{1,2},{2,3},{3,0},{4,5},{5,6},{6,7},{7,4},{8,9},{9,10},{10,1... | collective-permute-start | bytes 2150408 | tf_op jit(solution)/shard_map/ppermute | solution.py:20
  259.6 93.6 %all-to-all-start.3 = ((bf16[4,1120,280]{1,2,0:T(8,128)(2,1)}), bf16[4,1120,280]{1,2,0:T(8,128)(2,1)}, u32[]{:S(2)}, u32[]{:S(2)}) async-start(bf16[4,1120,280]{1,2,0:T(8,128)(2,1)} %copy.107), calls=%async_computation.3 | async-start | bytes 5160960 | tf_op jit(solution)/shard_map/all_to_all | solution.py:181
  264.2 168.2 %reduce-scatter.16.cloned.1.call-start = ((), (), s32[]{:S(2)}) async-start(), calls=%async_computation.18 | async-start | bytes 7372800 | tf_op jit(solution)/shard_map/reduce_scatter | solution.py:248
  264.2 44.7 %collective-permute-start.1 = (bf16[1,320,1120]{2,1,0:T(8,128)(2,1)S(1)}, bf16[1,320,1120]{2,1,0:T(8,128)(2,1)}, u32[]{:S(2)}, u32[]{:S(2)}) collective-permute-start(bf16[1,320,1120]{2,1,0:T(8,128)(2,1)S(1)} %copy-done.9), channel_id=1, source_target_pairs={{0,3},{1,0},{2,1},{3,2},{4,7},{5,4},{6,5},{7,6},{8,11},{9,8},{10,9... | collective-permute-start | bytes 2150408 | tf_op jit(solution)/shard_map/ppermute | solution.py:23
  269.7 63.3 %collective-permute-start.2 = (bf16[1,320,1120]{2,1,0:T(8,128)(2,1)}, bf16[1,320,1120]{2,1,0:T(8,128)(2,1)}, u32[]{:S(2)}, u32[]{:S(2)}) collective-permute-start(bf16[1,320,1120]{2,1,0:T(8,128)(2,1)} %collective-permute-done), channel_id=1, source_target_pairs={{0,1},{1,2},{2,3},{3,0},{4,5},{5,6},{6,7},{7,4},{8,9},{9,10},{10,1... | collective-permute-start | bytes 2150408 | tf_op jit(solution)/shard_map/ppermute | solution.py:20
  375.2 97.2 %reduce-scatter.14.cloned.1.call-start = ((), (), s32[]{:S(2)}) async-start(), calls=%async_computation.17 | async-start | bytes 3686400 | tf_op jit(solution)/shard_map/reduce_scatter | solution.py:229
  386.1 557.4 %reduce-scatter.24.cloned.1.call-start = ((), (), s32[]{:S(2)}) async-start(), calls=%async_computation.24 | async-start | bytes 6451200
  434.3 42.6 %copy-start.6 = (bf16[1,4,320,5,56]{2,4,3,1,0:T(8,128)(2,1)S(1)}, bf16[1,4,320,5,56]{2,4,3,1,0:T(8,128)(2,1)}, u32[]{:S(2)}) copy-start(bf16[1,4,320,5,56]{2,4,3,1,0:T(8,128)(2,1)} %copy.103) | copy-start | bytes 2150404
  485.1 15.9 %all-to-all-start.4 = ((bf16[1,320,20,56]{1,3,0,2:T(8,128)(2,1)}), bf16[1,320,20,56]{1,3,0,2:T(8,128)(2,1)S(1)}, u32[]{:S(2)}, u32[]{:S(2)}) async-start(bf16[1,320,20,56]{1,3,0,2:T(8,128)(2,1)} %bitcast.51), calls=%async_computation.6 | async-start | bytes 1720320 | tf_op jit(solution)/shard_map/all_to_all | solution.py:267
  488.6 454.9 %reduce-scatter.18.cloned.1.call-start = ((), (), s32[]{:S(2)}) async-start(), calls=%async_computation.19 | async-start | bytes 19353600 | tf_op jit(solution)/shard_map/reduce_scatter | solution.py:277
  525.1 17.6 %copy-start.2 = (bf16[1,1280,5,3,56]{1,4,2,3,0:T(8,128)(2,1)S(1)}, bf16[1,1280,5,3,56]{1,4,2,3,0:T(8,128)(2,1)}, u32[]{:S(2)}) copy-start(bf16[1,1280,5,3,56]{1,4,2,3,0:T(8,128)(2,1)} %copy-done.1) | copy-start | bytes 6451204
  695.5 12.8 copy-start.27
  695.5 12.8 copy-start.29
  728.6 308.1 %reduce-scatter.22.cloned.1.call-start = ((), (), s32[]{:S(2)}) async-start(), calls=%async_computation.23 | async-start | bytes 7741440
  841.1 325.4 %reduce-scatter.20.cloned.1.call-start = ((), (), s32[]{:S(2)}) async-start(), calls=%async_computation.22 | async-start | bytes 7741440
  943.2 408.4 %all-reduce.8.cloned.1.call-start = ((), (), s32[]{:S(2)}) async-start(), calls=%async_computation.25 | async-start | bytes 10321920 | tf_op jit(solution)/shard_map/psum | solution.py:281
  (24 other events, 147.4 us)
Sparse Core Ops, SparseCore 0:
  9.6 57.3 all-gather.8
  68.5 34.0 all-gather.10
  104.8 57.7 all-gather.14
  164.7 56.1 all-gather.16
  222.8 41.0 all-gather.12
  375.3 56.9 reduce-scatter.15
  435.7 36.7 reduce-scatter.13
  480.9 50.8 reduce-scatter.23
  728.7 175.8 reduce-scatter.17
  908.5 128.1 reduce-scatter.21
  1040.8 125.5 reduce-scatter.19
  1170.4 181.1 all-reduce.7
